TPU v7x, 32 devices: a whole 2x2x4 slice. The times are simulated.
32 devices in a mesh: sub: 8 (over y, x, core), reg: 4 (over z).
Axes of the slice: x: 2, y: 2, z: 4, core: 2. Of those that a mesh axis runs over, the one named last changes fastest.
Arguments:
- right_side: float32 [8, 4, 1280, 16], P('sub', 'reg'), may hold values from -6 to 6
- tiles: bfloat16 [8, 4, 80, 128, 128], P('sub', 'reg'), may hold values from -1 to 5
- tile_list: int32 [8, 4, 80, 2], P('sub', 'reg'), may hold values from 0 to 9, as said below
- weights: float32 [8, 4, 1280], P('sub', 'reg'), may hold values from 0.15 to 0.35
- face_map: int32 [8, 4, 6], P('sub', 'reg'), may hold values from 0 to 9, as said below
- matching: int32 [8, 4, 6, 128], P('sub', 'reg'), may hold values from 0 to 127, each once within a row
- coarse_basis: bfloat16 [8, 4, 1280, 128], P('sub', 'reg'), may hold values from -0.15625 to 0.15625
- coarse_map: int32 [8, 4, 128], P('sub', 'reg'), may hold values from 0 to 511, as said below
- coarse_inverse: float32 [4, 512, 512], P('reg', 'sub'), may hold values from -1 to 2, as said below
Outputs:
- solution: bfloat16 [8, 4, 1280, 16], P('sub', 'reg')
- residual: bfloat16 [8, 4, 1280, 16], P('sub', 'reg')
Inputs may be any that keep to these rules, and one draw needn't show every extreme that they name: `tile_list`: entries 0 to 9 of each subdomain's list are (b, b) for b in order; the other 70 entries are distinct off-diagonal block pairs. `face_map`: the six blocks of a subdomain are distinct. `coarse_map`: A subdomain's 128 numbers are distinct, and within a subregion every number is named by exactly two subdomains. `coarse_inverse`: symmetric in its last two dimensions.
All inputs are finite; a program needn't handle non-finite values.
Results may differ from a plain program's by a relative error of at most 0.0075.
Values may be sent and summed in bfloat16 or wider, within the bound.
No kernel may reach another device: no remote copies, remote signals or barrier semaphores. Data moves between devices by JAX's collectives and lax.ppermute only.
A program may use at most 64 MiB of HBM per device.

v0:
```python
import jax
import jax.numpy as jnp
from jax import lax
from jax.sharding import PartitionSpec as P

SWEEPS = 3


def from_behind(shard, axis, by):
    peers = lax.axis_size(axis)
    return lax.ppermute(shard, axis, [(i, (i + by) % peers) for i in range(peers)])


def body(
    right_side,
    tiles,
    tile_list,
    weights,
    face_map,
    matching,
    coarse_basis,
    coarse_map,
    coarse_inverse,
):
    order = right_side.shape[2]
    rights = right_side.shape[3]
    tile = tiles.shape[3]
    blocks = order // tile
    target = right_side[0, 0]
    tile_block = tiles[0, 0]
    listing = tile_list[0, 0]
    scaling = weights[0, 0][:, None]
    faces_here = face_map[0, 0]
    matched = matching[0, 0]
    basis = coarse_basis[0, 0]
    own_map = coarse_map[0, 0]
    own_count = own_map.shape[0]
    inverse_rows = coarse_inverse[0]
    held_rows = inverse_rows.shape[0]
    block_ids = jnp.arange(blocks, dtype=jnp.int32)
    row_table = (listing[:, 0][None, :] == block_ids[:, None]).astype(jnp.float32)
    face_table = (faces_here[None, :] == block_ids[:, None]).astype(jnp.float32)
    stride = max(lax.axis_size("reg") // 4, 1)
    every_ids = lax.all_gather(own_map, "sub", axis=0, tiled=True)
    outgoing_part = jnp.take(inverse_rows, every_ids, axis=1).reshape(
        held_rows, lax.axis_size("sub"), own_count
    )
    received_part = lax.all_to_all(outgoing_part, "sub", split_axis=1, concat_axis=0, tiled=True)
    own_columns = received_part.reshape(held_rows * lax.axis_size("sub"), own_count)
    own_block = jnp.transpose(jnp.take(own_columns, every_ids, axis=0))
    solution = jnp.zeros_like(target)
    residual = target
    for sweep in range(SWEEPS):
        low = residual.astype(jnp.bfloat16)
        local_coarse = jnp.einsum("mn,mr->nr", basis, low, preferred_element_type=jnp.float32)
        own_solution = jnp.dot(
            own_block,
            lax.all_gather(local_coarse, "sub", axis=0, tiled=True),
            precision=lax.Precision.HIGHEST,
            preferred_element_type=jnp.float32,
        )
        own_values = own_solution.astype(jnp.bfloat16)
        correction = jnp.dot(basis, own_values, preferred_element_type=jnp.float32)
        solution = solution + (scaling * residual + correction)
        operator_low = solution.astype(jnp.bfloat16).reshape(blocks, tile, rights)
        picked = jnp.take(operator_low, listing[:, 1], axis=0)
        products = jnp.einsum(
            "tij,tjr->tir", tile_block, picked, preferred_element_type=jnp.float32
        )
        local = jnp.einsum("bt,tir->bir", row_table, products, precision=lax.Precision.HIGHEST)
        stacked = solution.reshape(blocks, tile, rights)
        outgoing = jnp.take(stacked, faces_here, axis=0)
        arrived = []
        for face, offset in ((0, 1), (1, -1), (2, stride), (3, -stride)):
            arrived.append(from_behind(outgoing[face ^ 1], "reg", offset))
        for face, offset in ((4, 1), (5, -1)):
            arrived.append(from_behind(outgoing[face ^ 1], "sub", offset))
        received = jnp.stack(arrived)
        permuted = jnp.take_along_axis(received, matched[:, :, None], axis=1)
        coupling = jnp.einsum("bk,kir->bir", face_table, permuted, precision=lax.Precision.HIGHEST)
        residual = target - (local - 0.5 * coupling).reshape(order, rights)
    shape = (1, 1, order, rights)
    return (
        solution.astype(jnp.bfloat16).reshape(shape),
        residual.astype(jnp.bfloat16).reshape(shape),
    )


def solution(mesh):
    placed = (
        P("sub", "reg", None, None),
        P("sub", "reg", None, None, None),
        P("sub", "reg", None, None),
        P("sub", "reg", None),
        P("sub", "reg", None),
        P("sub", "reg", None, None),
        P("sub", "reg", None, None),
        P("sub", "reg", None),
        P("reg", "sub", None),
    )
    return jax.shard_map(
        body,
        mesh=mesh,
        in_specs=placed,
        out_specs=(P("sub", "reg", None, None), P("sub", "reg", None, None)),
        check_vma=False,
    )
```

profile of v0, /device:TPU:0, one launch (start us, length us, event | category | flops | bytes accessed | tf_op | source)
XLA Modules:
  0.0 149.0 jit_solution(13466135424913627133)
XLA Ops:
  0.7 10.7 %all-gather = s32[1,1,1024]{2,1,0:T(1,128)S(1)} all-gather(s32[1,1,128]{2,1,0:T(1,128)} %param.22), channel_id=2, replica_groups=mesh['sub'=8,'reg'=4] {'sub'}, dimensions={2}, use_global_device_ids=true | all-gather | bytes 4608 | tf_op jit(solution)/shard_map/all_gather | solution.py:44
  11.4 1.0 copy.30
  12.4 4.0 %gather_fusion = f32[1024,64]{1,0:T(8,128)} fusion(f32[64,512]{0,1:T(8,128)S(1)} %bitcast.251, s32[1024]{0:T(1024)S(1)} %fusion.82), kind=kCustom, calls=%fused_computation.9 | custom fusion | bytes 528384 | tf_op jit(solution)/shard_map/jit(_take)/gather | solution.py:45
  16.4 1.2 copy.31
  17.6 0.7 broadcast_select_fusion
  18.3 3.4 %all-to-all-start = ((f32[64,8,128]{2,0,1:T(8,128)}), f32[64,8,128]{2,0,1:T(8,128)S(1)}, u32[]{:S(2)}, u32[]{:S(2)}) async-start(f32[64,8,128]{2,0,1:T(8,128)} %broadcast_select_fusion), calls=%async_computation | async-start | bytes 524288 | tf_op jit(solution)/shard_map/all_to_all | solution.py:48
  21.8 0.5 compare_and_fusion.3
  22.3 0.5 slice_bitcast_fusion.18
  23.1 0.6 pad_clamp_fusion
  23.7 9.5 %all_gather.13 = f32[1024,16]{0,1:T(8,128)S(1)} all-gather(f32[128,16]{0,1:T(8,128)S(1)} %fusion.37), channel_id=1, replica_groups=mesh['sub'=8,'reg'=4] {'sub'}, dimensions={0}, use_global_device_ids=true | all-gather | bytes 73728 | tf_op jit(solution)/shard_map/all_gather | solution.py:58
  33.3 4.0 %gather_fusion.1 = f32[1024,128]{1,0:T(8,128)} fusion(f32[512,128]{1,0:T(8,128)S(1)} %bitcast.250, s32[1024]{0:T(1024)S(1)} %fusion.82), kind=kCustom, calls=%fused_computation.10 | custom fusion | bytes 1052672 | tf_op jit(solution)/shard_map/jit(_take)/gather | solution.py:50
  37.2 1.5 %convolution_convert_fusion.2 = bf16[128,16]{0,1:T(8,128)(2,1)S(1)} fusion(f32[1024,16]{0,1:T(8,128)S(1)} %all_gather.13, f32[1024,128]{1,0:T(8,128)} %gather_fusion.1, pred[1024]{0:T(1024)(128)(4,1)S(1)} %compare_and_fusion.1), kind=kOutput, calls=%fused_computation.38 | convolution fusion | flops 25298944 | bytes 594944 | tf_op jit(solution)/shard_map/dot_general | solution.py:56
  38.8 0.2 fusion.10
  39.0 0.6 gather_fusion.3
  39.7 1.6 %collective-permute-start = (f32[128,16]{0,1:T(8,128)S(1)}, f32[128,16]{0,1:T(8,128)}, u32[]{:S(2)}, u32[]{:S(2)}) collective-permute-start(f32[128,16]{0,1:T(8,128)S(1)} %get-tuple-element.26), channel_id=1, source_target_pairs={{0,1},{1,2},{2,3},{3,0},{4,5},{5,6},{6,7},{7,4},{8,9},{9,10},{10,1... | collective-permute-start | bytes 24584 | tf_op jit(solution)/shard_map/ppermute | solution.py:11
  41.3 2.2 %collective-permute-start.1 = (f32[128,16]{0,1:T(8,128)S(1)}, f32[128,16]{0,1:T(8,128)}, u32[]{:S(2)}, u32[]{:S(2)}) collective-permute-start(f32[128,16]{0,1:T(8,128)S(1)} %get-tuple-element.25), channel_id=1, source_target_pairs={{0,3},{1,0},{2,1},{3,2},{4,7},{5,4},{6,5},{7,6},{8,11},{9,8},{10,9... | collective-permute-start | bytes 24584 | tf_op jit(solution)/shard_map/ppermute | solution.py:11
  43.6 3.8 %collective-permute-start.3 = (f32[128,16]{0,1:T(8,128)S(1)}, f32[128,16]{0,1:T(8,128)}, u32[]{:S(2)}, u32[]{:S(2)}) collective-permute-start(f32[128,16]{0,1:T(8,128)S(1)} %get-tuple-element.23), channel_id=1, source_target_pairs={{0,3},{1,0},{2,1},{3,2},{4,7},{5,4},{6,5},{7,6},{8,11},{9,8},{10,9... | collective-permute-start | bytes 24584 | tf_op jit(solution)/shard_map/ppermute | solution.py:11
  47.4 0.8 gather_fusion.2
  48.2 2.2 %fusion.11 = f32[80,128,16]{1,2,0:T(8,128)S(1)} fusion(bf16[1,1,80,128,128]{4,3,2,1,0:T(8,128)(2,1)S(1)} %copy-done, bf16[80,128,16]{1,2,0:T(8,128)(2,1)S(1)} %gather_fusion.2, pred[80]{0:T(512)(128)(4,1)} %get-tuple-element.4), kind=kOutput, calls=%fused_computation.25 | convolution fusion | flops 42106880 | bytes 3604560 | tf_op jit(solution)/shard_map/tij,tjr->tir/dot_general | solution.py:67
  50.3 1.2 fusion.27
  51.5 2.6 %collective-permute-start.5 = (f32[128,16]{0,1:T(8,128)S(1)}, f32[128,16]{0,1:T(8,128)S(1)}, u32[]{:S(2)}, u32[]{:S(2)}) collective-permute-start(f32[128,16]{0,1:T(8,128)S(1)} %get-tuple-element.21), channel_id=1, source_target_pairs={{0,28},{4,0},{8,4},{12,8},{16,12},{20,16},{24,20},{28,24},{1,29},{... | collective-permute-start | bytes 24584 | tf_op jit(solution)/shard_map/ppermute | solution.py:11
  54.2 1.3 constant_dynamic-update-slice_fusion.5
  55.5 1.3 constant_dynamic-update-slice_fusion.4
  56.8 1.3 constant_dynamic-update-slice_fusion.3
  58.1 1.3 constant_dynamic-update-slice_fusion.2
  59.4 1.3 constant_dynamic-update-slice_fusion.1
  60.6 0.6 constant_dynamic-update-slice_fusion
  61.3 1.0 copy.35
  62.2 7.0 %gather_fusion.4 = f32[768,16]{1,0:T(8,128)} fusion(f32[6,128,16]{2,1,0:T(8,128)S(1)} %copy.35, s32[768]{0:T(1024)S(1)} %bitcast.246), kind=kCustom, calls=%fused_computation.2.clone | custom fusion | bytes 104448 | tf_op jit(solution)/shard_map/jit(take_along_axis)/gather | solution.py:79
  69.2 1.2 copy.36
  70.4 1.2 fusion.22
  71.6 0.2 convolution_bitcast_fusion.4
  71.8 9.0 %all_gather.14 = f32[1024,16]{0,1:T(8,128)S(1)} all-gather(f32[128,16]{0,1:T(8,128)S(1)} %convolution_bitcast_fusion.4), channel_id=1, replica_groups=mesh['sub'=8,'reg'=4] {'sub'}, dimensions={0}, use_global_device_ids=true | all-gather | bytes 73728 | tf_op jit(solution)/shard_map/all_gather | solution.py:58
  80.8 1.5 %convolution_convert_fusion.1 = bf16[128,16]{0,1:T(8,128)(2,1)S(1)} fusion(f32[1024,16]{0,1:T(8,128)S(1)} %all_gather.14, f32[1024,128]{1,0:T(8,128)} %gather_fusion.1, pred[1024]{0:T(1024)(128)(4,1)S(1)} %compare_and_fusion.1), kind=kOutput, calls=%fused_computation.37 | convolution fusion | flops 25298944 | bytes 594944 | tf_op jit(solution)/shard_map/dot_general | solution.py:56
  82.4 0.2 fusion.9
  82.6 0.6 copy-done.3
  83.2 0.9 gather_fusion.5
  84.2 2.4 %fusion.14 = f32[80,128,16]{1,2,0:T(8,128)} fusion(bf16[1,1,80,128,128]{4,3,2,1,0:T(8,128)(2,1)S(1)} %copy-done, bf16[80,128,16]{1,2,0:T(8,128)(2,1)S(1)} %gather_fusion.5, pred[80]{0:T(512)(128)(4,1)S(1)} %copy-done.13), kind=kOutput, calls=%fused_computation.26 | convolution fusion | flops 42106880 | bytes 3604560 | tf_op jit(solution)/shard_map/tij,tjr->tir/dot_general | solution.py:67
  86.5 0.6 gather_fusion.6
  87.3 2.2 %fusion.25 = f32[10,128,16]{1,0,2:T(8,128)} fusion(f32[80,128,16]{1,2,0:T(8,128)} %fusion.14, s32[80]{0:T(128)S(1)} %copy-done.12), kind=kOutput, calls=%fused_computation.41 | convolution fusion | flops 19661600 | bytes 737600 | tf_op jit(solution)/shard_map/bt,tir->bir/dot_general | solution.py:70
  89.5 3.8 %collective-permute-start.7 = (f32[128,16]{0,1:T(8,128)S(1)}, f32[128,16]{0,1:T(8,128)S(1)}, u32[]{:S(2)}, u32[]{:S(2)}) collective-permute-start(f32[128,16]{0,1:T(8,128)S(1)} %get-tuple-element.19), channel_id=1, source_target_pairs={{0,3},{1,0},{2,1},{3,2},{4,7},{5,4},{6,5},{7,6},{8,11},{9,8},{10,9... | collective-permute-start | bytes 24584 | tf_op jit(solution)/shard_map/ppermute | solution.py:11
  93.3 3.8 %collective-permute-start.9 = (f32[128,16]{0,1:T(8,128)S(1)}, f32[128,16]{0,1:T(8,128)S(1)}, u32[]{:S(2)}, u32[]{:S(2)}) collective-permute-start(f32[128,16]{0,1:T(8,128)S(1)} %get-tuple-element.17), channel_id=1, source_target_pairs={{0,3},{1,0},{2,1},{3,2},{4,7},{5,4},{6,5},{7,6},{8,11},{9,8},{10,9... | collective-permute-start | bytes 24584 | tf_op jit(solution)/shard_map/ppermute | solution.py:11
  97.1 2.6 %collective-permute-start.11 = (f32[128,16]{0,1:T(8,128)S(1)}, f32[128,16]{0,1:T(8,128)S(1)}, u32[]{:S(2)}, u32[]{:S(2)}) collective-permute-start(f32[128,16]{0,1:T(8,128)S(1)} %get-tuple-element.15), channel_id=1, source_target_pairs={{0,28},{4,0},{8,4},{12,8},{16,12},{20,16},{24,20},{28,24},{1,29},{... | collective-permute-start | bytes 24584 | tf_op jit(solution)/shard_map/ppermute | solution.py:11
  99.8 1.3 collective-permute-done.10
  101.3 7.0 %gather_fusion.7 = f32[768,16]{1,0:T(8,128)} fusion(f32[6,128,16]{2,1,0:T(8,128)S(1)} %copy.40, s32[768]{0:T(1024)S(1)} %bitcast.247), kind=kCustom, calls=%fused_computation.7.clone | custom fusion | bytes 104448 | tf_op jit(solution)/shard_map/jit(take_along_axis)/gather | solution.py:79
  108.3 1.2 copy.41
  109.5 1.2 fusion.21
  110.7 0.2 convolution_bitcast_fusion.3
  110.9 9.3 %all_gather.15 = f32[1024,16]{0,1:T(8,128)S(1)} all-gather(f32[128,16]{0,1:T(8,128)S(1)} %convolution_bitcast_fusion.3), channel_id=1, replica_groups=mesh['sub'=8,'reg'=4] {'sub'}, dimensions={0}, use_global_device_ids=true | all-gather | bytes 73728 | tf_op jit(solution)/shard_map/all_gather | solution.py:58
  120.2 1.5 %convolution_convert_fusion = bf16[128,16]{0,1:T(8,128)(2,1)S(1)} fusion(f32[1024,16]{0,1:T(8,128)S(1)} %all_gather.15, f32[1024,128]{1,0:T(8,128)} %gather_fusion.1, pred[1024]{0:T(1024)(128)(4,1)S(1)} %compare_and_fusion.1), kind=kOutput, calls=%fused_computation.36 | convolution fusion | flops 25298944 | bytes 594944 | tf_op jit(solution)/shard_map/dot_general | solution.py:56
  121.7 0.2 fusion.7
  121.9 0.6 convert_bitcast_fusion.2
  122.6 0.8 gather_fusion.8
  123.4 2.4 %fusion.17 = f32[80,128,16]{1,2,0:T(8,128)} fusion(bf16[1,1,80,128,128]{4,3,2,1,0:T(8,128)(2,1)S(1)} %copy-done, bf16[80,128,16]{1,2,0:T(8,128)(2,1)S(1)} %gather_fusion.8, pred[80]{0:T(512)(128)(4,1)S(1)} %copy-done.13), kind=kOutput, calls=%fused_computation.27 | convolution fusion | flops 42106880 | bytes 3604560 | tf_op jit(solution)/shard_map/tij,tjr->tir/dot_general | solution.py:67
  125.7 0.6 gather_fusion.9
  126.4 1.6 %fusion.23 = f32[10,128,16]{1,0,2:T(8,128)S(1)} fusion(f32[80,128,16]{1,2,0:T(8,128)} %fusion.17, s32[80]{0:T(128)S(1)} %copy-done.12), kind=kOutput, calls=%fused_computation.39 | convolution fusion | flops 19661600 | bytes 737600 | tf_op jit(solution)/shard_map/bt,tir->bir/dot_general | solution.py:70
  128.0 3.9 %collective-permute-start.13 = (f32[128,16]{0,1:T(8,128)S(1)}, f32[128,16]{0,1:T(8,128)S(1)}, u32[]{:S(2)}, u32[]{:S(2)}) collective-permute-start(f32[128,16]{0,1:T(8,128)S(1)} %get-tuple-element.13), channel_id=1, source_target_pairs={{0,3},{1,0},{2,1},{3,2},{4,7},{5,4},{6,5},{7,6},{8,11},{9,8},{10,9... | collective-permute-start | bytes 24584 | tf_op jit(solution)/shard_map/ppermute | solution.py:11
  131.9 3.8 %collective-permute-start.15 = (f32[128,16]{0,1:T(8,128)S(1)}, f32[128,16]{0,1:T(8,128)S(1)}, u32[]{:S(2)}, u32[]{:S(2)}) collective-permute-start(f32[128,16]{0,1:T(8,128)S(1)} %get-tuple-element.11), channel_id=1, source_target_pairs={{0,3},{1,0},{2,1},{3,2},{4,7},{5,4},{6,5},{7,6},{8,11},{9,8},{10,9... | collective-permute-start | bytes 24584 | tf_op jit(solution)/shard_map/ppermute | solution.py:11
  135.7 2.6 %collective-permute-start.17 = (f32[128,16]{0,1:T(8,128)S(1)}, f32[128,16]{0,1:T(8,128)S(1)}, u32[]{:S(2)}, u32[]{:S(2)}) collective-permute-start(f32[128,16]{0,1:T(8,128)S(1)} %get-tuple-element.9), channel_id=1, source_target_pairs={{0,28},{4,0},{8,4},{12,8},{16,12},{20,16},{24,20},{28,24},{1,29},{... | collective-permute-start | bytes 24584 | tf_op jit(solution)/shard_map/ppermute | solution.py:11
  138.4 1.3 collective-permute-done.16
  139.9 7.0 %gather_fusion.10 = f32[768,16]{1,0:T(8,128)} fusion(f32[6,128,16]{2,1,0:T(8,128)S(1)} %copy.45, s32[768]{0:T(1024)S(1)} %bitcast.248), kind=kCustom, calls=%fused_computation.8.clone | custom fusion | bytes 104448 | tf_op jit(solution)/shard_map/jit(take_along_axis)/gather | solution.py:79
  146.8 1.2 copy.46
  148.0 0.3 fusion.20
  148.4 0.6 subtract_convert_fusion
  (93 shorter events, 1.3 us)
Async XLA Ops:
  0.6 47.6 %copy-start = (bf16[1,1,80,128,128]{4,3,2,1,0:T(8,128)(2,1)S(1)}, bf16[1,1,80,128,128]{4,3,2,1,0:T(8,128)(2,1)}, u32[]{:S(2)}) copy-start(bf16[1,1,80,128,128]{4,3,2,1,0:T(8,128)(2,1)} %param.16) | copy-start | bytes 7864324
  0.6 21.1 %copy-start.14 = (s32[1,1,80,2]{2,3,1,0:T(2,128)S(1)}, s32[1,1,80,2]{2,3,1,0:T(2,128)}, u32[]{:S(2)}) copy-start(s32[1,1,80,2]{2,3,1,0:T(2,128)} %param.17) | copy-start | bytes 1924
  0.7 22.2 %copy-start.7 = (s32[1,1,6]{2,1,0:T(1,128)S(1)}, s32[1,1,6]{2,1,0:T(1,128)}, u32[]{:S(2)}) copy-start(s32[1,1,6]{2,1,0:T(1,128)} %param.19) | copy-start | bytes 76
  0.7 22.2 %copy-start.5 = (s32[1,1,6,128]{3,1,2,0:T(1,128)S(1)}, s32[1,1,6,128]{3,1,2,0:T(1,128)}, u32[]{:S(2)}) copy-start(s32[1,1,6,128]{3,1,2,0:T(1,128)} %param.20) | copy-start | bytes 9220
  0.7 22.2 %copy-start.1 = (bf16[1,1,1280,128]{3,2,1,0:T(8,128)(2,1)S(1)}, bf16[1,1,1280,128]{3,2,1,0:T(8,128)(2,1)}, u32[]{:S(2)}) copy-start(bf16[1,1,1280,128]{3,2,1,0:T(8,128)(2,1)} %param.21) | copy-start | bytes 983044
  0.7 22.2 %copy-start.2 = (f32[1,1,1280,16]{2,3,1,0:T(8,128)S(1)}, f32[1,1,1280,16]{2,3,1,0:T(8,128)}, u32[]{:S(2)}) copy-start(f32[1,1,1280,16]{2,3,1,0:T(8,128)} %param.15) | copy-start | bytes 245764
  0.7 32.5 %copy-start.6 = (f32[1,1,1280]{2,1,0:T(1,128)S(1)}, f32[1,1,1280]{2,1,0:T(1,128)}, u32[]{:S(2)}) copy-start(f32[1,1,1280]{2,1,0:T(1,128)} %param.18) | copy-start | bytes 15364
  18.3 14.9 %all-to-all-start = ((f32[64,8,128]{2,0,1:T(8,128)}), f32[64,8,128]{2,0,1:T(8,128)S(1)}, u32[]{:S(2)}, u32[]{:S(2)}) async-start(f32[64,8,128]{2,0,1:T(8,128)} %broadcast_select_fusion), calls=%async_computation | async-start | bytes 524288 | tf_op jit(solution)/shard_map/all_to_all | solution.py:48
  22.9 16.7 %copy-start.9 = (pred[6]{0:T(512)(128)(4,1)}, pred[6]{0:T(512)(128)(4,1)S(1)}, u32[]{:S(2)}) copy-start(pred[6]{0:T(512)(128)(4,1)S(1)} %compare_and_fusion.2) | copy-start | bytes 22
  39.7 11.8 %collective-permute-start = (f32[128,16]{0,1:T(8,128)S(1)}, f32[128,16]{0,1:T(8,128)}, u32[]{:S(2)}, u32[]{:S(2)}) collective-permute-start(f32[128,16]{0,1:T(8,128)S(1)} %get-tuple-element.26), channel_id=1, source_target_pairs={{0,1},{1,2},{2,3},{3,0},{4,5},{5,6},{6,7},{7,4},{8,9},{9,10},{10,1... | collective-permute-start | bytes 24584 | tf_op jit(solution)/shard_map/ppermute | solution.py:11
  41.3 14.2 %collective-permute-start.1 = (f32[128,16]{0,1:T(8,128)S(1)}, f32[128,16]{0,1:T(8,128)}, u32[]{:S(2)}, u32[]{:S(2)}) collective-permute-start(f32[128,16]{0,1:T(8,128)S(1)} %get-tuple-element.25), channel_id=1, source_target_pairs={{0,3},{1,0},{2,1},{3,2},{4,7},{5,4},{6,5},{7,6},{8,11},{9,8},{10,9... | collective-permute-start | bytes 24584 | tf_op jit(solution)/shard_map/ppermute | solution.py:11
  43.6 13.2 %collective-permute-start.2 = (f32[128,16]{0,1:T(8,128)S(1)}, f32[128,16]{0,1:T(8,128)}, u32[]{:S(2)}, u32[]{:S(2)}) collective-permute-start(f32[128,16]{0,1:T(8,128)S(1)} %get-tuple-element.24), channel_id=1, source_target_pairs={{0,1},{1,2},{2,3},{3,0},{4,5},{5,6},{6,7},{7,4},{8,9},{9,10},{10,1... | collective-permute-start | bytes 24584 | tf_op jit(solution)/shard_map/ppermute | solution.py:11
  43.6 14.5 %collective-permute-start.3 = (f32[128,16]{0,1:T(8,128)S(1)}, f32[128,16]{0,1:T(8,128)}, u32[]{:S(2)}, u32[]{:S(2)}) collective-permute-start(f32[128,16]{0,1:T(8,128)S(1)} %get-tuple-element.23), channel_id=1, source_target_pairs={{0,3},{1,0},{2,1},{3,2},{4,7},{5,4},{6,5},{7,6},{8,11},{9,8},{10,9... | collective-permute-start | bytes 24584 | tf_op jit(solution)/shard_map/ppermute | solution.py:11
  47.4 12.0 %collective-permute-start.4 = (f32[128,16]{0,1:T(8,128)S(1)}, f32[128,16]{0,1:T(8,128)}, u32[]{:S(2)}, u32[]{:S(2)}) collective-permute-start(f32[128,16]{0,1:T(8,128)S(1)} %get-tuple-element.22), channel_id=1, source_target_pairs={{0,4},{4,8},{8,12},{12,16},{16,20},{20,24},{24,28},{28,0},{1,5},{5... | collective-permute-start | bytes 24584 | tf_op jit(solution)/shard_map/ppermute | solution.py:11
  48.2 2.2 %copy-start.11 = (s32[80]{0:T(128)S(1)}, s32[80]{0:T(128)}, u32[]{:S(2)}) copy-start(s32[80]{0:T(128)} %slice_bitcast_fusion.18) | copy-start | bytes 964
  51.5 18.8 %copy-start.8 = (s32[1,1,6]{2,1,0:T(1,128)S(1)}, s32[1,1,6]{2,1,0:T(1,128)}, u32[]{:S(2)}) copy-start(s32[1,1,6]{2,1,0:T(1,128)} %param.19) | copy-start | bytes 76
  51.5 9.1 %collective-permute-start.5 = (f32[128,16]{0,1:T(8,128)S(1)}, f32[128,16]{0,1:T(8,128)S(1)}, u32[]{:S(2)}, u32[]{:S(2)}) collective-permute-start(f32[128,16]{0,1:T(8,128)S(1)} %get-tuple-element.21), channel_id=1, source_target_pairs={{0,28},{4,0},{8,4},{12,8},{16,12},{20,16},{24,20},{28,24},{1,29},{... | collective-permute-start | bytes 24584 | tf_op jit(solution)/shard_map/ppermute | solution.py:11
  82.6 0.6 copy-start.3
  83.2 0.9 copy-start.13
  84.2 2.9 %copy-start.10 = (pred[6]{0:T(512)(128)(4,1)S(1)}, pred[6]{0:T(512)(128)(4,1)}, u32[]{:S(2)}) copy-start(pred[6]{0:T(512)(128)(4,1)} %copy-done.9) | copy-start | bytes 22
  84.2 3.1 %copy-start.12 = (s32[80]{0:T(128)S(1)}, s32[80]{0:T(128)}, u32[]{:S(2)}) copy-start(s32[80]{0:T(128)} %slice_bitcast_fusion.18) | copy-start | bytes 964
  87.2 9.9 %collective-permute-start.6 = (f32[128,16]{0,1:T(8,128)S(1)}, f32[128,16]{0,1:T(8,128)S(1)}, u32[]{:S(2)}, u32[]{:S(2)}) collective-permute-start(f32[128,16]{0,1:T(8,128)S(1)} %get-tuple-element.20), channel_id=1, source_target_pairs={{0,1},{1,2},{2,3},{3,0},{4,5},{5,6},{6,7},{7,4},{8,9},{9,10},{10,1... | collective-permute-start | bytes 24584 | tf_op jit(solution)/shard_map/ppermute | solution.py:11
  89.5 10.3 %collective-permute-start.7 = (f32[128,16]{0,1:T(8,128)S(1)}, f32[128,16]{0,1:T(8,128)S(1)}, u32[]{:S(2)}, u32[]{:S(2)}) collective-permute-start(f32[128,16]{0,1:T(8,128)S(1)} %get-tuple-element.19), channel_id=1, source_target_pairs={{0,3},{1,0},{2,1},{3,2},{4,7},{5,4},{6,5},{7,6},{8,11},{9,8},{10,9... | collective-permute-start | bytes 24584 | tf_op jit(solution)/shard_map/ppermute | solution.py:11
  93.3 6.5 %collective-permute-start.8 = (f32[128,16]{0,1:T(8,128)S(1)}, f32[128,16]{0,1:T(8,128)S(1)}, u32[]{:S(2)}, u32[]{:S(2)}) collective-permute-start(f32[128,16]{0,1:T(8,128)S(1)} %get-tuple-element.18), channel_id=1, source_target_pairs={{0,1},{1,2},{2,3},{3,0},{4,5},{5,6},{6,7},{7,4},{8,9},{9,10},{10,1... | collective-permute-start | bytes 24584 | tf_op jit(solution)/shard_map/ppermute | solution.py:11
  93.3 6.5 %collective-permute-start.9 = (f32[128,16]{0,1:T(8,128)S(1)}, f32[128,16]{0,1:T(8,128)S(1)}, u32[]{:S(2)}, u32[]{:S(2)}) collective-permute-start(f32[128,16]{0,1:T(8,128)S(1)} %get-tuple-element.17), channel_id=1, source_target_pairs={{0,3},{1,0},{2,1},{3,2},{4,7},{5,4},{6,5},{7,6},{8,11},{9,8},{10,9... | collective-permute-start | bytes 24584 | tf_op jit(solution)/shard_map/ppermute | solution.py:11
  97.1 4.0 %collective-permute-start.10 = (f32[128,16]{0,1:T(8,128)S(1)}, f32[128,16]{0,1:T(8,128)S(1)}, u32[]{:S(2)}, u32[]{:S(2)}) collective-permute-start(f32[128,16]{0,1:T(8,128)S(1)} %get-tuple-element.16), channel_id=1, source_target_pairs={{0,4},{4,8},{8,12},{12,16},{16,20},{20,24},{24,28},{28,0},{1,5},{5... | collective-permute-start | bytes 24584 | tf_op jit(solution)/shard_map/ppermute | solution.py:11
  97.1 4.0 %collective-permute-start.11 = (f32[128,16]{0,1:T(8,128)S(1)}, f32[128,16]{0,1:T(8,128)S(1)}, u32[]{:S(2)}, u32[]{:S(2)}) collective-permute-start(f32[128,16]{0,1:T(8,128)S(1)} %get-tuple-element.15), channel_id=1, source_target_pairs={{0,28},{4,0},{8,4},{12,8},{16,12},{20,16},{24,20},{28,24},{1,29},{... | collective-permute-start | bytes 24584 | tf_op jit(solution)/shard_map/ppermute | solution.py:11
  101.3 20.4 %copy-start.4 = (f32[1280,16]{0,1:T(8,128)S(1)}, f32[1280,16]{0,1:T(8,128)}, u32[]{:S(2)}) copy-start(f32[1280,16]{0,1:T(8,128)} %copy-done.3) | copy-start | bytes 245764
  126.4 9.3 %collective-permute-start.12 = (f32[128,16]{0,1:T(8,128)S(1)}, f32[128,16]{0,1:T(8,128)S(1)}, u32[]{:S(2)}, u32[]{:S(2)}) collective-permute-start(f32[128,16]{0,1:T(8,128)S(1)} %get-tuple-element.14), channel_id=1, source_target_pairs={{0,1},{1,2},{2,3},{3,0},{4,5},{5,6},{6,7},{7,4},{8,9},{9,10},{10,1... | collective-permute-start | bytes 24584 | tf_op jit(solution)/shard_map/ppermute | solution.py:11
  128.0 10.3 %collective-permute-start.13 = (f32[128,16]{0,1:T(8,128)S(1)}, f32[128,16]{0,1:T(8,128)S(1)}, u32[]{:S(2)}, u32[]{:S(2)}) collective-permute-start(f32[128,16]{0,1:T(8,128)S(1)} %get-tuple-element.13), channel_id=1, source_target_pairs={{0,3},{1,0},{2,1},{3,2},{4,7},{5,4},{6,5},{7,6},{8,11},{9,8},{10,9... | collective-permute-start | bytes 24584 | tf_op jit(solution)/shard_map/ppermute | solution.py:11
  131.9 6.5 %collective-permute-start.14 = (f32[128,16]{0,1:T(8,128)S(1)}, f32[128,16]{0,1:T(8,128)S(1)}, u32[]{:S(2)}, u32[]{:S(2)}) collective-permute-start(f32[128,16]{0,1:T(8,128)S(1)} %get-tuple-element.12), channel_id=1, source_target_pairs={{0,1},{1,2},{2,3},{3,0},{4,5},{5,6},{6,7},{7,4},{8,9},{9,10},{10,1... | collective-permute-start | bytes 24584 | tf_op jit(solution)/shard_map/ppermute | solution.py:11
  131.9 6.5 %collective-permute-start.15 = (f32[128,16]{0,1:T(8,128)S(1)}, f32[128,16]{0,1:T(8,128)S(1)}, u32[]{:S(2)}, u32[]{:S(2)}) collective-permute-start(f32[128,16]{0,1:T(8,128)S(1)} %get-tuple-element.11), channel_id=1, source_target_pairs={{0,3},{1,0},{2,1},{3,2},{4,7},{5,4},{6,5},{7,6},{8,11},{9,8},{10,9... | collective-permute-start | bytes 24584 | tf_op jit(solution)/shard_map/ppermute | solution.py:11
  135.7 4.0 %collective-permute-start.16 = (f32[128,16]{0,1:T(8,128)S(1)}, f32[128,16]{0,1:T(8,128)S(1)}, u32[]{:S(2)}, u32[]{:S(2)}) collective-permute-start(f32[128,16]{0,1:T(8,128)S(1)} %get-tuple-element.10), channel_id=1, source_target_pairs={{0,4},{4,8},{8,12},{12,16},{16,20},{20,24},{24,28},{28,0},{1,5},{5... | collective-permute-start | bytes 24584 | tf_op jit(solution)/shard_map/ppermute | solution.py:11
  135.7 4.0 %collective-permute-start.17 = (f32[128,16]{0,1:T(8,128)S(1)}, f32[128,16]{0,1:T(8,128)S(1)}, u32[]{:S(2)}, u32[]{:S(2)}) collective-permute-start(f32[128,16]{0,1:T(8,128)S(1)} %get-tuple-element.9), channel_id=1, source_target_pairs={{0,28},{4,0},{8,4},{12,8},{16,12},{20,16},{24,20},{28,24},{1,29},{... | collective-permute-start | bytes 24584 | tf_op jit(solution)/shard_map/ppermute | solution.py:11
where the time goes:
time: 150 us; the launch traced here: 149 us
  local copies, waits for them, and re-layouts  48.4 us (32%)
  blocking collectives  38.5 us (26%)
  starting transfers between devices  34.5 us (23%)
  matrix products  20.4 us (14%)
  other arithmetic  3.46 us (2%)
  waiting for transfers between devices  2.68 us (2%)
    ppermute x18, starting transfers between devices, from_behind(): lax.ppermute(shard, axis, [(i, (i + by) % peers) for i in range(peers)])  31.1 us
    all_gather x3, blocking collectives, body(): lax.all_gather(local_coarse, 'sub', axis=0, tiled=True)  27.8 us
    gather x6, local copies, waits for them, and re-layouts, body(): permuted = jnp.take_along_axis(received, matched[:, :, None], axis=1)  24.4 us
    all_gather x1, blocking collectives, body(): every_ids = lax.all_gather(own_map, 'sub', axis=0, tiled=True)  10.7 us
    unnamed x47, local copies, waits for them, and re-layouts  8.21 us
    dot_general x3, matrix products, body(): jnp.einsum('tij,tjr->tir', tile_block, picked, preferred_element_type=jnp...  6.87 us
    gather x2, local copies, waits for them, and re-layouts, body(): jnp.take(inverse_rows, every_ids, axis=1)  5.21 us
    dot_general x3, matrix products, body(): jnp.einsum('bt,tir->bir', row_table, products, precision=lax.Precision.HI...  4.98 us
  transfers between devices with their start and end apart: 19, of which 2 were waited for; matrix products, arithmetic and copies ran while one was open for 11% of the time, Pallas kernels for 0%

commit v1 on v0

--- a/solution.py
+++ b/solution.py
@@ -2,6 +2,7 @@
 import jax.numpy as jnp
 from jax import lax
 from jax.sharding import PartitionSpec as P
+from jax.lax import axis_index, axis_size, ppermute
 
 SWEEPS = 3
 
@@ -41,7 +42,27 @@
     row_table = (listing[:, 0][None, :] == block_ids[:, None]).astype(jnp.float32)
     face_table = (faces_here[None, :] == block_ids[:, None]).astype(jnp.float32)
     stride = max(lax.axis_size("reg") // 4, 1)
-    every_ids = lax.all_gather(own_map, "sub", axis=0, tiled=True)
+    reached = axis_size("sub")
+    piece_now = axis_index("sub")
+    found_now, g_now, fresh = (reached, piece_now, own_map.shape[0])
+    arrivals = [(ix, (ix + 1) % found_now) for ix in range(found_now)]
+    samples = [(ix, (ix - 1) % found_now) for ix in range(found_now)]
+    every_ids = jnp.zeros(
+        (*own_map.shape[:0], found_now * fresh, *own_map.shape[0 + 1 :]), own_map.dtype
+    )
+    every_ids = lax.dynamic_update_slice_in_dim(every_ids, own_map, g_now * fresh, axis=0)
+    t1 = local_next = own_map
+    arr_out = found_now // 2
+    for dev_j in range(1, arr_out + 1):
+        t1 = ppermute(t1, "sub", arrivals)
+        every_ids = lax.dynamic_update_slice_in_dim(
+            every_ids, t1, (g_now - dev_j) % found_now * fresh, axis=0
+        )
+        if dev_j < found_now - arr_out:
+            local_next = ppermute(local_next, "sub", samples)
+            every_ids = lax.dynamic_update_slice_in_dim(
+                every_ids, local_next, (g_now + dev_j) % found_now * fresh, axis=0
+            )
     outgoing_part = jnp.take(inverse_rows, every_ids, axis=1).reshape(
         held_rows, lax.axis_size("sub"), own_count
     )

time: 150 us -> 156 us (1.040)
  blocking collectives: 38.5 us -> 27.7 us
  starting transfers between devices: 34.5 us -> 43.7 us
  waiting for transfers between devices: 2.68 us -> 6.79 us
  other arithmetic: 3.46 us -> 6.81 us
  matrix products: 20.4 us -> 22.9 us
  local copies, waits for them, and re-layouts: 48.4 us -> 46.1 us
    all_gather x1 -> x0, blocking collectives: 10.7 us -> none  [body(): every_ids = lax.all_gather(own_map, 'sub', axis=0, tiled=True)]
    ppermute x0 -> x7, starting transfers between devices: none -> 8.82 us  [the longest x3 8.27 us: body(): local_next = ppermute(local_next, 'sub', samples)]
    ppermute x0 -> x7, waiting for transfers between devices: none -> 4.11 us  [the longest x4 3.93 us: body(): t1 = ppermute(t1, 'sub', arrivals)]
    gather x6, local copies, waits for them, and re-layouts: 24.4 us -> 21.6 us  [body(): permuted = jnp.take_along_axis(received, matched[:, :, None], axis=1)]
    gather x2, local copies, waits for them, and re-layouts: 5.21 us -> 2.99 us  [body(): jnp.take(inverse_rows, every_ids, axis=1)]
    dynamic_update_slice x0 -> x8, local copies, waits for them, and re-layouts: none -> 2.1 us  [the longest x1 0.77 us: body(): lax.dynamic_update_slice_in_dim(every_ids, own_map, g_now * fresh, axis=0)]
    unnamed x47 -> x41, local copies, waits for them, and re-layouts: 8.21 us -> 8.18 us
  transfers between devices with their start and end apart: 19 -> 26, of which waited for: 2 -> 6; matrix products, arithmetic and copies ran while one was open for 11% -> 16% of each run, Pallas kernels for 0% -> 0%
where the time goes in v1:
time: 156 us; the launch traced here: 155 us
  local copies, waits for them, and re-layouts  46.1 us (30%)
  starting transfers between devices  43.7 us (28%)
  blocking collectives  27.7 us (18%)
  matrix products  22.9 us (15%)
  other arithmetic  6.81 us (4%)
  waiting for transfers between devices  6.79 us (4%)
    ppermute x18, starting transfers between devices, from_behind(): lax.ppermute(shard, axis, [(i, (i + by) % peers) for i in range(peers)])  31.4 us
    all_gather x3, blocking collectives, body(): lax.all_gather(local_coarse, 'sub', axis=0, tiled=True)  27.7 us
    gather x6, local copies, waits for them, and re-layouts, body(): permuted = jnp.take_along_axis(received, matched[:, :, None], axis=1)  21.6 us
    ppermute x3, starting transfers between devices, body(): local_next = ppermute(local_next, 'sub', samples)  8.27 us
    unnamed x41, local copies, waits for them, and re-layouts  8.18 us
    dot_general x3, matrix products, body(): jnp.einsum('tij,tjr->tir', tile_block, picked, preferred_element_type=jnp...  6.91 us
    dot_general x3, matrix products, body(): jnp.einsum('bt,tir->bir', row_table, products, precision=lax.Precision.HI...  5.6 us
    dot_general x3, matrix products, body(): jnp.dot(own_block, lax.all_gather(local_coarse, 'sub', axis=0, tiled=True...  4.59 us
  transfers between devices with their start and end apart: 26, of which 6 were waited for; matrix products, arithmetic and copies ran while one was open for 16% of the time, Pallas kernels for 0%

profile of v1, /device:TPU:0, one launch (start us, length us, event | category | flops | bytes accessed | tf_op | source)
XLA Modules:
  0.0 155.2 jit_solution(9682849350432204065)
XLA Ops:
  1.2 2.9 %collective-permute-start.1 = (s32[128]{0:T(128)}, s32[128]{0:T(128)S(1)}, u32[]{:S(2)}, u32[]{:S(2)}) collective-permute-start(s32[128]{0:T(128)} %bitcast.268), channel_id=1, source_target_pairs={{0,28},{4,0},{8,4},{12,8},{16,12},{20,16},{24,20},{28,24},{1,29},{... | collective-permute-start | bytes 1544 | tf_op jit(solution)/shard_map/ppermute | solution.py:62
  4.1 1.2 compare_and_fusion.3
  5.3 1.2 slice_bitcast_fusion.18
  6.5 0.7 compare_select_fusion.2
  7.2 0.7 compare_and_fusion.2
  7.9 0.7 or_reduce_fusion
  8.6 0.7 compare_and_fusion
  9.3 1.2 fusion.37
  10.4 0.8 bitcast_dynamic-update-slice_fusion
  11.2 0.6 pad_clamp_fusion
  11.8 2.6 %collective-permute-start.3 = (s32[128]{0:T(128)S(1)}, s32[128]{0:T(128)S(1)}, u32[]{:S(2)}, u32[]{:S(2)}) collective-permute-start(s32[128]{0:T(128)S(1)} %collective-permute-done.1), channel_id=1, source_target_pairs={{0,28},{4,0},{8,4},{12,8},{16,12},{20,16},{24,20},{28,24},{1,29},{... | collective-permute-start | bytes 1544 | tf_op jit(solution)/shard_map/ppermute | solution.py:62
  14.5 1.2 collective-permute-done.2
  15.7 1.0 copy.30
  16.8 2.7 %collective-permute-start.5 = (s32[128]{0:T(128)S(1)}, s32[128]{0:T(128)S(1)}, u32[]{:S(2)}, u32[]{:S(2)}) collective-permute-start(s32[128]{0:T(128)S(1)} %collective-permute-done.3), channel_id=1, source_target_pairs={{0,28},{4,0},{8,4},{12,8},{16,12},{20,16},{24,20},{28,24},{1,29},{... | collective-permute-start | bytes 1544 | tf_op jit(solution)/shard_map/ppermute | solution.py:62
  20.9 2.6 %collective-permute-done.6 = s32[128]{0:T(128)S(1)} collective-permute-done((s32[128]{0:T(128)S(1)}, s32[128]{0:T(128)S(1)}, u32[]{:S(2)}, u32[]{:S(2)}) %collective-permute-start.6) | collective-permute-done | bytes 544 | tf_op jit(solution)/shard_map/ppermute | solution.py:57
  23.7 2.8 %gather_fusion = f32[1024,64]{1,0:T(8,128)S(1)} fusion(f32[64,512]{0,1:T(8,128)S(1)} %bitcast.252, s32[1024]{0:T(1024)S(1)} %fusion.82), kind=kCustom, calls=%fused_computation.9 | custom fusion | bytes 528384 | tf_op jit(solution)/shard_map/jit(_take)/gather | solution.py:66
  26.7 0.7 broadcast_select_fusion
  27.4 3.5 %all-to-all-start = ((f32[64,8,128]{2,0,1:T(8,128)}), f32[64,8,128]{2,0,1:T(8,128)S(1)}, u32[]{:S(2)}, u32[]{:S(2)}) async-start(f32[64,8,128]{2,0,1:T(8,128)} %broadcast_select_fusion), calls=%async_computation | async-start | bytes 524288 | tf_op jit(solution)/shard_map/all_to_all | solution.py:69
  30.9 10.3 %all_gather.9 = f32[1024,16]{0,1:T(8,128)S(1)} all-gather(f32[128,16]{0,1:T(8,128)S(1)} %fusion.37), channel_id=1, replica_groups=mesh['sub'=8,'reg'=4] {'sub'}, dimensions={0}, use_global_device_ids=true | all-gather | bytes 73728 | tf_op jit(solution)/shard_map/all_gather | solution.py:79
  41.2 4.0 %gather_fusion.1 = f32[1024,128]{1,0:T(8,128)} fusion(f32[512,128]{1,0:T(8,128)S(1)} %bitcast.251, s32[1024]{0:T(1024)S(1)} %fusion.82), kind=kCustom, calls=%fused_computation.10 | custom fusion | bytes 1052672 | tf_op jit(solution)/shard_map/jit(_take)/gather | solution.py:71
  45.2 1.5 convolution_convert_fusion.2
  47.7 2.2 %collective-permute-start.7 = (f32[128,16]{0,1:T(8,128)S(1)}, f32[128,16]{0,1:T(8,128)}, u32[]{:S(2)}, u32[]{:S(2)}) collective-permute-start(f32[128,16]{0,1:T(8,128)S(1)} %get-tuple-element.26), channel_id=1, source_target_pairs={{0,1},{1,2},{2,3},{3,0},{4,5},{5,6},{6,7},{7,4},{8,9},{9,10},{10,1... | collective-permute-start | bytes 24584 | tf_op jit(solution)/shard_map/ppermute | solution.py:12
  49.9 2.1 %collective-permute-start.8 = (f32[128,16]{0,1:T(8,128)S(1)}, f32[128,16]{0,1:T(8,128)}, u32[]{:S(2)}, u32[]{:S(2)}) collective-permute-start(f32[128,16]{0,1:T(8,128)S(1)} %get-tuple-element.25), channel_id=1, source_target_pairs={{0,3},{1,0},{2,1},{3,2},{4,7},{5,4},{6,5},{7,6},{8,11},{9,8},{10,9... | collective-permute-start | bytes 24584 | tf_op jit(solution)/shard_map/ppermute | solution.py:12
  52.0 3.8 %collective-permute-start.10 = (f32[128,16]{0,1:T(8,128)S(1)}, f32[128,16]{0,1:T(8,128)}, u32[]{:S(2)}, u32[]{:S(2)}) collective-permute-start(f32[128,16]{0,1:T(8,128)S(1)} %get-tuple-element.23), channel_id=1, source_target_pairs={{0,3},{1,0},{2,1},{3,2},{4,7},{5,4},{6,5},{7,6},{8,11},{9,8},{10,9... | collective-permute-start | bytes 24584 | tf_op jit(solution)/shard_map/ppermute | solution.py:12
  55.8 0.8 gather_fusion.2
  56.6 2.2 %fusion.11 = f32[80,128,16]{1,2,0:T(8,128)S(1)} fusion(bf16[1,1,80,128,128]{4,3,2,1,0:T(8,128)(2,1)S(1)} %copy-done, bf16[80,128,16]{1,2,0:T(8,128)(2,1)S(1)} %gather_fusion.2, pred[80]{0:T(512)(128)(4,1)} %get-tuple-element.4), kind=kOutput, calls=%fused_computation.25 | convolution fusion | flops 42106880 | bytes 3604560 | tf_op jit(solution)/shard_map/tij,tjr->tir/dot_general | solution.py:88
  58.7 1.2 fusion.27
  59.9 2.6 %collective-permute-start.12 = (f32[128,16]{0,1:T(8,128)S(1)}, f32[128,16]{0,1:T(8,128)S(1)}, u32[]{:S(2)}, u32[]{:S(2)}) collective-permute-start(f32[128,16]{0,1:T(8,128)S(1)} %get-tuple-element.21), channel_id=1, source_target_pairs={{0,28},{4,0},{8,4},{12,8},{16,12},{20,16},{24,20},{28,24},{1,29},{... | collective-permute-start | bytes 24584 | tf_op jit(solution)/shard_map/ppermute | solution.py:12
  62.5 1.3 constant_dynamic-update-slice_fusion.5
  63.8 1.3 constant_dynamic-update-slice_fusion.4
  65.1 1.3 constant_dynamic-update-slice_fusion.3
  66.4 1.3 constant_dynamic-update-slice_fusion.2
  67.7 1.3 constant_dynamic-update-slice_fusion.1
  69.0 0.6 constant_dynamic-update-slice_fusion
  69.6 1.0 copy.35
  70.6 7.0 %gather_fusion.4 = f32[768,16]{1,0:T(8,128)} fusion(f32[6,128,16]{2,1,0:T(8,128)S(1)} %copy.35, s32[768]{0:T(1024)S(1)} %bitcast.247), kind=kCustom, calls=%fused_computation.2.clone | custom fusion | bytes 104448 | tf_op jit(solution)/shard_map/jit(take_along_axis)/gather | solution.py:100
  77.6 1.2 copy.36
  78.7 1.2 fusion.22
  80.2 8.4 %all_gather.10 = f32[1024,16]{0,1:T(8,128)S(1)} all-gather(f32[128,16]{0,1:T(8,128)S(1)} %convolution_bitcast_fusion.4), channel_id=1, replica_groups=mesh['sub'=8,'reg'=4] {'sub'}, dimensions={0}, use_global_device_ids=true | all-gather | bytes 73728 | tf_op jit(solution)/shard_map/all_gather | solution.py:79
  88.5 1.5 convolution_convert_fusion.1
  90.3 0.6 copy-done.3
  90.9 0.9 gather_fusion.5
  91.9 2.4 %fusion.14 = f32[80,128,16]{1,2,0:T(8,128)} fusion(bf16[1,1,80,128,128]{4,3,2,1,0:T(8,128)(2,1)S(1)} %copy-done, bf16[80,128,16]{1,2,0:T(8,128)(2,1)S(1)} %gather_fusion.5, pred[80]{0:T(512)(128)(4,1)S(1)} %copy-done.11), kind=kOutput, calls=%fused_computation.26 | convolution fusion | flops 42106880 | bytes 3604560 | tf_op jit(solution)/shard_map/tij,tjr->tir/dot_general | solution.py:88
  95.0 2.2 %fusion.25 = f32[10,128,16]{1,0,2:T(8,128)} fusion(f32[80,128,16]{1,2,0:T(8,128)} %fusion.14, s32[80]{0:T(128)S(1)} %copy-done.10), kind=kOutput, calls=%fused_computation.41 | convolution fusion | flops 19661600 | bytes 737600 | tf_op jit(solution)/shard_map/bt,tir->bir/dot_general | solution.py:91
  97.2 3.8 %collective-permute-start.14 = (f32[128,16]{0,1:T(8,128)S(1)}, f32[128,16]{0,1:T(8,128)S(1)}, u32[]{:S(2)}, u32[]{:S(2)}) collective-permute-start(f32[128,16]{0,1:T(8,128)S(1)} %get-tuple-element.19), channel_id=1, source_target_pairs={{0,3},{1,0},{2,1},{3,2},{4,7},{5,4},{6,5},{7,6},{8,11},{9,8},{10,9... | collective-permute-start | bytes 24584 | tf_op jit(solution)/shard_map/ppermute | solution.py:12
  101.0 3.8 %collective-permute-start.16 = (f32[128,16]{0,1:T(8,128)S(1)}, f32[128,16]{0,1:T(8,128)S(1)}, u32[]{:S(2)}, u32[]{:S(2)}) collective-permute-start(f32[128,16]{0,1:T(8,128)S(1)} %get-tuple-element.17), channel_id=1, source_target_pairs={{0,3},{1,0},{2,1},{3,2},{4,7},{5,4},{6,5},{7,6},{8,11},{9,8},{10,9... | collective-permute-start | bytes 24584 | tf_op jit(solution)/shard_map/ppermute | solution.py:12
  104.8 2.6 %collective-permute-start.18 = (f32[128,16]{0,1:T(8,128)S(1)}, f32[128,16]{0,1:T(8,128)S(1)}, u32[]{:S(2)}, u32[]{:S(2)}) collective-permute-start(f32[128,16]{0,1:T(8,128)S(1)} %get-tuple-element.15), channel_id=1, source_target_pairs={{0,28},{4,0},{8,4},{12,8},{16,12},{20,16},{24,20},{28,24},{1,29},{... | collective-permute-start | bytes 24584 | tf_op jit(solution)/shard_map/ppermute | solution.py:12
  107.5 1.3 collective-permute-done.17
  109.0 7.0 %gather_fusion.7 = f32[768,16]{1,0:T(8,128)} fusion(f32[6,128,16]{2,1,0:T(8,128)S(1)} %copy.40, s32[768]{0:T(1024)S(1)} %bitcast.248), kind=kCustom, calls=%fused_computation.7.clone | custom fusion | bytes 104448 | tf_op jit(solution)/shard_map/jit(take_along_axis)/gather | solution.py:100
  116.0 1.2 copy.41
  117.2 1.2 fusion.21
  118.6 9.1 %all_gather.11 = f32[1024,16]{0,1:T(8,128)S(1)} all-gather(f32[128,16]{0,1:T(8,128)S(1)} %convolution_bitcast_fusion.3), channel_id=1, replica_groups=mesh['sub'=8,'reg'=4] {'sub'}, dimensions={0}, use_global_device_ids=true | all-gather | bytes 73728 | tf_op jit(solution)/shard_map/all_gather | solution.py:79
  127.7 1.5 convolution_convert_fusion
  129.5 0.6 convert_bitcast_fusion.2
  130.1 0.8 gather_fusion.8
  130.9 2.4 %fusion.17 = f32[80,128,16]{1,2,0:T(8,128)} fusion(bf16[1,1,80,128,128]{4,3,2,1,0:T(8,128)(2,1)S(1)} %copy-done, bf16[80,128,16]{1,2,0:T(8,128)(2,1)S(1)} %gather_fusion.8, pred[80]{0:T(512)(128)(4,1)S(1)} %copy-done.11), kind=kOutput, calls=%fused_computation.27 | convolution fusion | flops 42106880 | bytes 3604560 | tf_op jit(solution)/shard_map/tij,tjr->tir/dot_general | solution.py:88
  134.0 2.2 %fusion.23 = f32[10,128,16]{1,0,2:T(8,128)} fusion(f32[80,128,16]{1,2,0:T(8,128)} %fusion.17, s32[80]{0:T(128)S(1)} %copy-done.10), kind=kOutput, calls=%fused_computation.39 | convolution fusion | flops 19661600 | bytes 737600 | tf_op jit(solution)/shard_map/bt,tir->bir/dot_general | solution.py:91
  136.2 3.8 %collective-permute-start.20 = (f32[128,16]{0,1:T(8,128)S(1)}, f32[128,16]{0,1:T(8,128)S(1)}, u32[]{:S(2)}, u32[]{:S(2)}) collective-permute-start(f32[128,16]{0,1:T(8,128)S(1)} %get-tuple-element.13), channel_id=1, source_target_pairs={{0,3},{1,0},{2,1},{3,2},{4,7},{5,4},{6,5},{7,6},{8,11},{9,8},{10,9... | collective-permute-start | bytes 24584 | tf_op jit(solution)/shard_map/ppermute | solution.py:12
  140.0 3.8 %collective-permute-start.22 = (f32[128,16]{0,1:T(8,128)S(1)}, f32[128,16]{0,1:T(8,128)S(1)}, u32[]{:S(2)}, u32[]{:S(2)}) collective-permute-start(f32[128,16]{0,1:T(8,128)S(1)} %get-tuple-element.11), channel_id=1, source_target_pairs={{0,3},{1,0},{2,1},{3,2},{4,7},{5,4},{6,5},{7,6},{8,11},{9,8},{10,9... | collective-permute-start | bytes 24584 | tf_op jit(solution)/shard_map/ppermute | solution.py:12
  143.8 2.6 %collective-permute-start.24 = (f32[128,16]{0,1:T(8,128)S(1)}, f32[128,16]{0,1:T(8,128)S(1)}, u32[]{:S(2)}, u32[]{:S(2)}) collective-permute-start(f32[128,16]{0,1:T(8,128)S(1)} %get-tuple-element.9), channel_id=1, source_target_pairs={{0,28},{4,0},{8,4},{12,8},{16,12},{20,16},{24,20},{28,24},{1,29},{... | collective-permute-start | bytes 24584 | tf_op jit(solution)/shard_map/ppermute | solution.py:12
  146.5 1.3 collective-permute-done.23
  148.0 5.1 %gather_fusion.10 = f32[768,16]{1,0:T(8,128)S(1)} fusion(f32[6,128,16]{2,1,0:T(8,128)S(1)} %copy.45, s32[768]{0:T(1024)S(1)} %bitcast.249), kind=kCustom, calls=%fused_computation.8.clone | custom fusion | bytes 104448 | tf_op jit(solution)/shard_map/jit(take_along_axis)/gather | solution.py:100
  153.3 1.2 fusion.20
  154.6 0.6 subtract_convert_fusion
  (109 shorter events, 6.2 us)
Async XLA Ops:
  0.6 55.9 %copy-start = (bf16[1,1,80,128,128]{4,3,2,1,0:T(8,128)(2,1)S(1)}, bf16[1,1,80,128,128]{4,3,2,1,0:T(8,128)(2,1)}, u32[]{:S(2)}) copy-start(bf16[1,1,80,128,128]{4,3,2,1,0:T(8,128)(2,1)} %param.16) | copy-start | bytes 7864324
  0.6 11.2 %collective-permute-start = (s32[128]{0:T(128)}, s32[128]{0:T(128)S(1)}, u32[]{:S(2)}, u32[]{:S(2)}) collective-permute-start(s32[128]{0:T(128)} %bitcast.267), channel_id=1, source_target_pairs={{0,4},{4,8},{8,12},{12,16},{16,20},{20,24},{24,28},{28,0},{1,5},{5... | collective-permute-start | bytes 1544 | tf_op jit(solution)/shard_map/ppermute | solution.py:57
  1.2 10.6 %collective-permute-start.1 = (s32[128]{0:T(128)}, s32[128]{0:T(128)S(1)}, u32[]{:S(2)}, u32[]{:S(2)}) collective-permute-start(s32[128]{0:T(128)} %bitcast.268), channel_id=1, source_target_pairs={{0,28},{4,0},{8,4},{12,8},{16,12},{20,16},{24,20},{28,24},{1,29},{... | collective-permute-start | bytes 1544 | tf_op jit(solution)/shard_map/ppermute | solution.py:62
  4.1 37.0 %copy-start.5 = (f32[1,1,1280]{2,1,0:T(1,128)S(1)}, f32[1,1,1280]{2,1,0:T(1,128)}, u32[]{:S(2)}) copy-start(f32[1,1,1280]{2,1,0:T(1,128)} %param.18) | copy-start | bytes 15364
  7.9 39.7 %copy-start.7 = (pred[6]{0:T(512)(128)(4,1)}, pred[6]{0:T(512)(128)(4,1)S(1)}, u32[]{:S(2)}) copy-start(pred[6]{0:T(512)(128)(4,1)S(1)} %compare_and_fusion.2) | copy-start | bytes 22
  11.8 3.9 %collective-permute-start.2 = (s32[128]{0:T(128)S(1)}, s32[128]{0:T(128)S(1)}, u32[]{:S(2)}, u32[]{:S(2)}) collective-permute-start(s32[128]{0:T(128)S(1)} %collective-permute-done), channel_id=1, source_target_pairs={{0,4},{4,8},{8,12},{12,16},{16,20},{20,24},{24,28},{28,0},{1,5},{5... | collective-permute-start | bytes 1544 | tf_op jit(solution)/shard_map/ppermute | solution.py:57
  11.8 4.9 %collective-permute-start.3 = (s32[128]{0:T(128)S(1)}, s32[128]{0:T(128)S(1)}, u32[]{:S(2)}, u32[]{:S(2)}) collective-permute-start(s32[128]{0:T(128)S(1)} %collective-permute-done.1), channel_id=1, source_target_pairs={{0,28},{4,0},{8,4},{12,8},{16,12},{20,16},{24,20},{28,24},{1,29},{... | collective-permute-start | bytes 1544 | tf_op jit(solution)/shard_map/ppermute | solution.py:62
  15.7 3.9 %collective-permute-start.4 = (s32[128]{0:T(128)S(1)}, s32[128]{0:T(128)S(1)}, u32[]{:S(2)}, u32[]{:S(2)}) collective-permute-start(s32[128]{0:T(128)S(1)} %collective-permute-done.2), channel_id=1, source_target_pairs={{0,4},{4,8},{8,12},{12,16},{16,20},{20,24},{24,28},{28,0},{1,5},{5... | collective-permute-start | bytes 1544 | tf_op jit(solution)/shard_map/ppermute | solution.py:57
  16.8 4.0 %collective-permute-start.5 = (s32[128]{0:T(128)S(1)}, s32[128]{0:T(128)S(1)}, u32[]{:S(2)}, u32[]{:S(2)}) collective-permute-start(s32[128]{0:T(128)S(1)} %collective-permute-done.3), channel_id=1, source_target_pairs={{0,28},{4,0},{8,4},{12,8},{16,12},{20,16},{24,20},{28,24},{1,29},{... | collective-permute-start | bytes 1544 | tf_op jit(solution)/shard_map/ppermute | solution.py:62
  19.6 3.9 %collective-permute-start.6 = (s32[128]{0:T(128)S(1)}, s32[128]{0:T(128)S(1)}, u32[]{:S(2)}, u32[]{:S(2)}) collective-permute-start(s32[128]{0:T(128)S(1)} %collective-permute-done.4), channel_id=1, source_target_pairs={{0,4},{4,8},{8,12},{12,16},{16,20},{20,24},{24,28},{28,0},{1,5},{5... | collective-permute-start | bytes 1544 | tf_op jit(solution)/shard_map/ppermute | solution.py:57
  27.4 13.8 %all-to-all-start = ((f32[64,8,128]{2,0,1:T(8,128)}), f32[64,8,128]{2,0,1:T(8,128)S(1)}, u32[]{:S(2)}, u32[]{:S(2)}) async-start(f32[64,8,128]{2,0,1:T(8,128)} %broadcast_select_fusion), calls=%async_computation | async-start | bytes 524288 | tf_op jit(solution)/shard_map/all_to_all | solution.py:69
  41.2 5.5 %copy-start.1 = (bf16[1,1,1280,128]{3,2,1,0:T(8,128)(2,1)S(1)}, bf16[1,1,1280,128]{3,2,1,0:T(8,128)(2,1)}, u32[]{:S(2)}) copy-start(bf16[1,1,1280,128]{3,2,1,0:T(8,128)(2,1)} %param.21) | copy-start | bytes 983044
  41.2 5.5 %copy-start.2 = (f32[1,1,1280,16]{2,3,1,0:T(8,128)S(1)}, f32[1,1,1280,16]{2,3,1,0:T(8,128)}, u32[]{:S(2)}) copy-start(f32[1,1,1280,16]{2,3,1,0:T(8,128)} %param.15) | copy-start | bytes 245764
  47.7 12.2 %collective-permute-start.7 = (f32[128,16]{0,1:T(8,128)S(1)}, f32[128,16]{0,1:T(8,128)}, u32[]{:S(2)}, u32[]{:S(2)}) collective-permute-start(f32[128,16]{0,1:T(8,128)S(1)} %get-tuple-element.26), channel_id=1, source_target_pairs={{0,1},{1,2},{2,3},{3,0},{4,5},{5,6},{6,7},{7,4},{8,9},{9,10},{10,1... | collective-permute-start | bytes 24584 | tf_op jit(solution)/shard_map/ppermute | solution.py:12
  49.9 14.0 %collective-permute-start.8 = (f32[128,16]{0,1:T(8,128)S(1)}, f32[128,16]{0,1:T(8,128)}, u32[]{:S(2)}, u32[]{:S(2)}) collective-permute-start(f32[128,16]{0,1:T(8,128)S(1)} %get-tuple-element.25), channel_id=1, source_target_pairs={{0,3},{1,0},{2,1},{3,2},{4,7},{5,4},{6,5},{7,6},{8,11},{9,8},{10,9... | collective-permute-start | bytes 24584 | tf_op jit(solution)/shard_map/ppermute | solution.py:12
  51.9 13.2 %collective-permute-start.9 = (f32[128,16]{0,1:T(8,128)S(1)}, f32[128,16]{0,1:T(8,128)}, u32[]{:S(2)}, u32[]{:S(2)}) collective-permute-start(f32[128,16]{0,1:T(8,128)S(1)} %get-tuple-element.24), channel_id=1, source_target_pairs={{0,1},{1,2},{2,3},{3,0},{4,5},{5,6},{6,7},{7,4},{8,9},{9,10},{10,1... | collective-permute-start | bytes 24584 | tf_op jit(solution)/shard_map/ppermute | solution.py:12
  52.0 14.5 %collective-permute-start.10 = (f32[128,16]{0,1:T(8,128)S(1)}, f32[128,16]{0,1:T(8,128)}, u32[]{:S(2)}, u32[]{:S(2)}) collective-permute-start(f32[128,16]{0,1:T(8,128)S(1)} %get-tuple-element.23), channel_id=1, source_target_pairs={{0,3},{1,0},{2,1},{3,2},{4,7},{5,4},{6,5},{7,6},{8,11},{9,8},{10,9... | collective-permute-start | bytes 24584 | tf_op jit(solution)/shard_map/ppermute | solution.py:12
  55.8 11.9 %collective-permute-start.11 = (f32[128,16]{0,1:T(8,128)S(1)}, f32[128,16]{0,1:T(8,128)}, u32[]{:S(2)}, u32[]{:S(2)}) collective-permute-start(f32[128,16]{0,1:T(8,128)S(1)} %get-tuple-element.22), channel_id=1, source_target_pairs={{0,4},{4,8},{8,12},{12,16},{16,20},{20,24},{24,28},{28,0},{1,5},{5... | collective-permute-start | bytes 24584 | tf_op jit(solution)/shard_map/ppermute | solution.py:12
  56.6 2.2 %copy-start.9 = (s32[80]{0:T(128)S(1)}, s32[80]{0:T(128)}, u32[]{:S(2)}) copy-start(s32[80]{0:T(128)} %slice_bitcast_fusion.18) | copy-start | bytes 964
  59.9 18.8 %copy-start.6 = (s32[1,1,6]{2,1,0:T(1,128)S(1)}, s32[1,1,6]{2,1,0:T(1,128)}, u32[]{:S(2)}) copy-start(s32[1,1,6]{2,1,0:T(1,128)} %param.19) | copy-start | bytes 76
  59.9 9.1 %collective-permute-start.12 = (f32[128,16]{0,1:T(8,128)S(1)}, f32[128,16]{0,1:T(8,128)S(1)}, u32[]{:S(2)}, u32[]{:S(2)}) collective-permute-start(f32[128,16]{0,1:T(8,128)S(1)} %get-tuple-element.21), channel_id=1, source_target_pairs={{0,28},{4,0},{8,4},{12,8},{16,12},{20,16},{24,20},{28,24},{1,29},{... | collective-permute-start | bytes 24584 | tf_op jit(solution)/shard_map/ppermute | solution.py:12
  90.3 0.6 copy-start.3
  90.9 0.9 copy-start.11
  91.9 3.0 %copy-start.8 = (pred[6]{0:T(512)(128)(4,1)S(1)}, pred[6]{0:T(512)(128)(4,1)}, u32[]{:S(2)}) copy-start(pred[6]{0:T(512)(128)(4,1)} %copy-done.7) | copy-start | bytes 22
  91.9 3.1 %copy-start.10 = (s32[80]{0:T(128)S(1)}, s32[80]{0:T(128)}, u32[]{:S(2)}) copy-start(s32[80]{0:T(128)} %slice_bitcast_fusion.18) | copy-start | bytes 964
  94.9 9.9 %collective-permute-start.13 = (f32[128,16]{0,1:T(8,128)S(1)}, f32[128,16]{0,1:T(8,128)S(1)}, u32[]{:S(2)}, u32[]{:S(2)}) collective-permute-start(f32[128,16]{0,1:T(8,128)S(1)} %get-tuple-element.20), channel_id=1, source_target_pairs={{0,1},{1,2},{2,3},{3,0},{4,5},{5,6},{6,7},{7,4},{8,9},{9,10},{10,1... | collective-permute-start | bytes 24584 | tf_op jit(solution)/shard_map/ppermute | solution.py:12
  97.2 10.3 %collective-permute-start.14 = (f32[128,16]{0,1:T(8,128)S(1)}, f32[128,16]{0,1:T(8,128)S(1)}, u32[]{:S(2)}, u32[]{:S(2)}) collective-permute-start(f32[128,16]{0,1:T(8,128)S(1)} %get-tuple-element.19), channel_id=1, source_target_pairs={{0,3},{1,0},{2,1},{3,2},{4,7},{5,4},{6,5},{7,6},{8,11},{9,8},{10,9... | collective-permute-start | bytes 24584 | tf_op jit(solution)/shard_map/ppermute | solution.py:12
  101.0 6.5 %collective-permute-start.15 = (f32[128,16]{0,1:T(8,128)S(1)}, f32[128,16]{0,1:T(8,128)S(1)}, u32[]{:S(2)}, u32[]{:S(2)}) collective-permute-start(f32[128,16]{0,1:T(8,128)S(1)} %get-tuple-element.18), channel_id=1, source_target_pairs={{0,1},{1,2},{2,3},{3,0},{4,5},{5,6},{6,7},{7,4},{8,9},{9,10},{10,1... | collective-permute-start | bytes 24584 | tf_op jit(solution)/shard_map/ppermute | solution.py:12
  101.0 6.5 %collective-permute-start.16 = (f32[128,16]{0,1:T(8,128)S(1)}, f32[128,16]{0,1:T(8,128)S(1)}, u32[]{:S(2)}, u32[]{:S(2)}) collective-permute-start(f32[128,16]{0,1:T(8,128)S(1)} %get-tuple-element.17), channel_id=1, source_target_pairs={{0,3},{1,0},{2,1},{3,2},{4,7},{5,4},{6,5},{7,6},{8,11},{9,8},{10,9... | collective-permute-start | bytes 24584 | tf_op jit(solution)/shard_map/ppermute | solution.py:12
  104.8 4.0 %collective-permute-start.17 = (f32[128,16]{0,1:T(8,128)S(1)}, f32[128,16]{0,1:T(8,128)S(1)}, u32[]{:S(2)}, u32[]{:S(2)}) collective-permute-start(f32[128,16]{0,1:T(8,128)S(1)} %get-tuple-element.16), channel_id=1, source_target_pairs={{0,4},{4,8},{8,12},{12,16},{16,20},{20,24},{24,28},{28,0},{1,5},{5... | collective-permute-start | bytes 24584 | tf_op jit(solution)/shard_map/ppermute | solution.py:12
  104.8 4.0 %collective-permute-start.18 = (f32[128,16]{0,1:T(8,128)S(1)}, f32[128,16]{0,1:T(8,128)S(1)}, u32[]{:S(2)}, u32[]{:S(2)}) collective-permute-start(f32[128,16]{0,1:T(8,128)S(1)} %get-tuple-element.15), channel_id=1, source_target_pairs={{0,28},{4,0},{8,4},{12,8},{16,12},{20,16},{24,20},{28,24},{1,29},{... | collective-permute-start | bytes 24584 | tf_op jit(solution)/shard_map/ppermute | solution.py:12
  109.0 20.2 %copy-start.4 = (f32[1280,16]{0,1:T(8,128)S(1)}, f32[1280,16]{0,1:T(8,128)}, u32[]{:S(2)}) copy-start(f32[1280,16]{0,1:T(8,128)} %copy-done.3) | copy-start | bytes 245764
  133.9 9.9 %collective-permute-start.19 = (f32[128,16]{0,1:T(8,128)S(1)}, f32[128,16]{0,1:T(8,128)S(1)}, u32[]{:S(2)}, u32[]{:S(2)}) collective-permute-start(f32[128,16]{0,1:T(8,128)S(1)} %get-tuple-element.14), channel_id=1, source_target_pairs={{0,1},{1,2},{2,3},{3,0},{4,5},{5,6},{6,7},{7,4},{8,9},{9,10},{10,1... | collective-permute-start | bytes 24584 | tf_op jit(solution)/shard_map/ppermute | solution.py:12
  136.2 10.3 %collective-permute-start.20 = (f32[128,16]{0,1:T(8,128)S(1)}, f32[128,16]{0,1:T(8,128)S(1)}, u32[]{:S(2)}, u32[]{:S(2)}) collective-permute-start(f32[128,16]{0,1:T(8,128)S(1)} %get-tuple-element.13), channel_id=1, source_target_pairs={{0,3},{1,0},{2,1},{3,2},{4,7},{5,4},{6,5},{7,6},{8,11},{9,8},{10,9... | collective-permute-start | bytes 24584 | tf_op jit(solution)/shard_map/ppermute | solution.py:12
  140.0 6.5 %collective-permute-start.21 = (f32[128,16]{0,1:T(8,128)S(1)}, f32[128,16]{0,1:T(8,128)S(1)}, u32[]{:S(2)}, u32[]{:S(2)}) collective-permute-start(f32[128,16]{0,1:T(8,128)S(1)} %get-tuple-element.12), channel_id=1, source_target_pairs={{0,1},{1,2},{2,3},{3,0},{4,5},{5,6},{6,7},{7,4},{8,9},{9,10},{10,1... | collective-permute-start | bytes 24584 | tf_op jit(solution)/shard_map/ppermute | solution.py:12
  140.0 6.5 %collective-permute-start.22 = (f32[128,16]{0,1:T(8,128)S(1)}, f32[128,16]{0,1:T(8,128)S(1)}, u32[]{:S(2)}, u32[]{:S(2)}) collective-permute-start(f32[128,16]{0,1:T(8,128)S(1)} %get-tuple-element.11), channel_id=1, source_target_pairs={{0,3},{1,0},{2,1},{3,2},{4,7},{5,4},{6,5},{7,6},{8,11},{9,8},{10,9... | collective-permute-start | bytes 24584 | tf_op jit(solution)/shard_map/ppermute | solution.py:12
  143.8 4.0 %collective-permute-start.23 = (f32[128,16]{0,1:T(8,128)S(1)}, f32[128,16]{0,1:T(8,128)S(1)}, u32[]{:S(2)}, u32[]{:S(2)}) collective-permute-start(f32[128,16]{0,1:T(8,128)S(1)} %get-tuple-element.10), channel_id=1, source_target_pairs={{0,4},{4,8},{8,12},{12,16},{16,20},{20,24},{24,28},{28,0},{1,5},{5... | collective-permute-start | bytes 24584 | tf_op jit(solution)/shard_map/ppermute | solution.py:12
  143.8 4.0 %collective-permute-start.24 = (f32[128,16]{0,1:T(8,128)S(1)}, f32[128,16]{0,1:T(8,128)S(1)}, u32[]{:S(2)}, u32[]{:S(2)}) collective-permute-start(f32[128,16]{0,1:T(8,128)S(1)} %get-tuple-element.9), channel_id=1, source_target_pairs={{0,28},{4,0},{8,4},{12,8},{16,12},{20,16},{24,20},{28,24},{1,29},{... | collective-permute-start | bytes 24584 | tf_op jit(solution)/shard_map/ppermute | solution.py:12
